TPU v7x, 32 devices: a whole 2x2x4 slice. The times are simulated.
32 devices in a mesh: grp: 4 (over z), ex: 8 (over y, x, core).
Axes of the slice: x: 2, y: 2, z: 4, core: 2. Of those that a mesh axis runs over, the one named last changes fastest.
Arguments:
- tokens: bfloat16 [2048, 3584], P(('grp', 'ex')), may hold values from -6 to 6
- expert_ids: int32 [2048, 8], P(('grp', 'ex')), may hold values from 0 to 15, all different within a row; in each aligned block of 64 rows (0 to 63, 64 to 127, ...) at most 40 rows name the same one
- combine: float32 [2048, 8], P(('grp', 'ex')), may hold values from 0.25 to 0.5
- hot_flags: int32 [16], replicated, may hold values from 0 to 1
- gate_up_weight: bfloat16 [4, 8, 2, 3584, 512], P('grp', 'ex'), as said below
- gate_up_scale: float32 [4, 8, 2, 28, 512], P('grp', 'ex')
- down_weight: bfloat16 [4, 8, 512, 3584], P('grp', 'ex'), as said below
- down_scale: float32 [4, 8, 4, 3584], P('grp', 'ex')
Outputs:
- moe_out: bfloat16 [2048, 3584], P(('grp', 'ex'))
Inputs may be any that keep to these rules, and one draw needn't show every extreme that they name: `expert_ids`: each row names 8 different experts; the 64 rows of one device name one expert at most 40 times. `gate_up_weight`: for an expert whose hot flag is 0, every entry is an integer from -8 to 7. `down_weight`: for an expert whose hot flag is 0, every entry is an integer from -8 to 7.
All inputs are finite; a program needn't handle non-finite values.
Results may differ from a plain program's by a relative error of at most 0.008.
Values may be sent and summed in bfloat16 or wider, within the bound.
A program may use at most 128 MiB of HBM per device.

v0:
```python
import jax
import jax.numpy as jnp
from jax import lax
from jax.sharding import PartitionSpec as P


def dequantize(weights, scales, is_hot):
    group_count = scales.shape[0]
    shaped = weights.reshape(group_count, weights.shape[0] // group_count, weights.shape[1])
    scaled = (shaped * scales[:, None, :]).reshape(weights.shape).astype(jnp.bfloat16)
    return jnp.where(is_hot, weights, scaled)


def shards(
    tokens, expert_ids, combine, hot_flags, gate_up_weight, gate_up_scale, down_weight, down_scale
):
    group_count = lax.axis_size("grp")
    lane_count = lax.axis_size("ex")
    pair_count = group_count // 2
    token_count = tokens.shape[0]
    model_width = tokens.shape[1]
    top_count = expert_ids.shape[1]
    expert_count = pair_count * lane_count
    route_count = token_count * top_count
    capacity = max(2, (5 * route_count + 4 * expert_count - 1) // (4 * expert_count))
    slot_count = expert_count * capacity
    flat_expert = expert_ids.reshape(route_count)
    route_order = jnp.arange(route_count, dtype=jnp.int32)
    earlier = (flat_expert[None, :] == flat_expert[:, None]) & (
        route_order[None, :] < route_order[:, None]
    )
    route_rank = jnp.sum(earlier, axis=1, dtype=jnp.int32)
    slot_of = flat_expert * capacity + route_rank
    slot_match = slot_of[None, :] == jnp.arange(slot_count, dtype=jnp.int32)[:, None]
    filled = jnp.any(slot_match, axis=1)
    source = jnp.sum(jnp.where(slot_match, route_order[None, :] // top_count, 0), axis=1)
    slot_rows = jnp.where(filled[:, None], tokens[source], jnp.zeros((), tokens.dtype))
    outgoing = slot_rows.reshape(pair_count, lane_count, capacity, model_width)
    own_expert = lax.axis_index("grp") // 2 * lane_count + lax.axis_index("ex")
    is_hot = hot_flags[own_expert] == 1
    gate_matrix = dequantize(gate_up_weight[0, 0, 0], gate_up_scale[0, 0, 0], is_hot)
    up_matrix = dequantize(gate_up_weight[0, 0, 1], gate_up_scale[0, 0, 1], is_hot)
    down_matrix = dequantize(down_weight[0, 0], down_scale[0, 0], is_hot)
    pair_index = flat_expert // lane_count
    lane_index = flat_expert % lane_count
    within = lax.all_to_all(outgoing, "ex", split_axis=1, concat_axis=1, tiled=True)
    doubled = jnp.repeat(within, 2, axis=0)
    arrived_block = lax.all_to_all(doubled, "grp", split_axis=0, concat_axis=0, tiled=True)
    flat_rows = arrived_block.reshape(-1, model_width)
    gate_proj = jnp.dot(flat_rows, gate_matrix, preferred_element_type=jnp.float32)
    up_proj = jnp.dot(flat_rows, up_matrix, preferred_element_type=jnp.float32)
    hidden = (jax.nn.silu(gate_proj) * up_proj).astype(jnp.bfloat16)
    partial_value = jnp.dot(hidden, down_matrix, preferred_element_type=jnp.float32).astype(
        jnp.bfloat16
    )
    across = lax.all_to_all(
        partial_value.reshape(arrived_block.shape), "grp", split_axis=0, concat_axis=0, tiled=True
    )
    returned = lax.all_to_all(across, "ex", split_axis=1, concat_axis=1, tiled=True)
    flat_back = returned.reshape(-1, model_width)
    first_index = (2 * pair_index * lane_count + lane_index) * capacity + route_rank
    second_index = first_index + lane_count * capacity
    both_halves = flat_back[first_index].astype(jnp.float32) + flat_back[second_index].astype(
        jnp.float32
    )
    expert_rows = lax.optimization_barrier(both_halves.astype(jnp.bfloat16)).astype(jnp.float32)
    weighted = expert_rows * combine.reshape(route_count)[:, None]
    return jnp.sum(weighted.reshape(token_count, top_count, model_width), axis=1).astype(
        jnp.bfloat16
    )


def solution(mesh):
    return jax.shard_map(
        shards,
        mesh=mesh,
        in_specs=(
            P(("grp", "ex"), None),
            P(("grp", "ex"), None),
            P(("grp", "ex"), None),
            P(),
            P("grp", "ex", None, None, None),
            P("grp", "ex", None, None, None),
            P("grp", "ex", None, None),
            P("grp", "ex", None, None),
        ),
        out_specs=P(("grp", "ex"), None),
        check_vma=False,
    )
```

profile of v0, /device:TPU:0, one launch (start us, length us, event | category | flops | bytes accessed | tf_op | source)
XLA Modules:
  0.0 669.1 jit_solution(5183161889637616623)
XLA Ops:
  0.0 0.8 copy.43
  1.8 5.1 gather_fusion
  6.9 2.7 copy_select_fusion
  9.6 58.2 %all_to_all.20 = bf16[2,8,40,3584]{3,2,0,1:T(8,128)(2,1)S(1)} all-to-all(bf16[2,8,40,3584]{3,2,0,1:T(8,128)(2,1)S(1)} %copy_select_fusion), channel_id=1, replica_groups=mesh['grp'=4,'ex'=8] {'ex'}, dimensions={1} | all-to-all | bytes 9175040 | tf_op jit(solution)/shard_map/all_to_all | solution.py:46
  67.8 2.5 copy.46
  70.3 6.6 broadcast_in_dim.43
  76.9 6.1 all-to-all-start.1
  83.0 0.6 dynamic_slice.3
  84.3 4.7 fusion.3
  89.2 193.7 %all-to-all-done.1 = bf16[4,8,40,3584]{3,2,1,0:T(8,128)(2,1)} async-done(((bf16[4,8,40,3584]{3,2,1,0:T(8,128)(2,1)}), bf16[4,8,40,3584]{3,2,1,0:T(8,128)(2,1)}, u32[]{:S(2)}, u32[]{:S(2)}) %all-to-all-start.1) | async-done | bytes 9175072 | tf_op jit(solution)/shard_map/all_to_all | solution.py:48
  282.9 0.9 mul.104
  283.8 8.6 %fusion.8 = f32[1280,512]{1,0:T(8,128)S(1)} fusion(bf16[1280,3584]{1,0:T(8,128)(2,1)} %bitcast.2, f32[1,1,1,3584,512]{4,3,2,1,0:T(8,128)S(1)} %bitcast.46, bf16[1,1,2,3584,512]{4,3,2,1,0:T(8,128)(2,1)} %param.12, pred[]{:T(512)} %bitcast.3), kind=kOutput, calls=%fused_computation.17 | convolution fusion | flops 4704960512 | bytes 22807040 | tf_op jit(solution)/shard_map/dot_general | solution.py:50
  292.4 0.9 mul.109
  293.3 10.3 %fusion.17 = bf16[1280,512]{1,0:T(8,128)(2,1)S(1)} fusion(bf16[1280,3584]{1,0:T(8,128)(2,1)} %bitcast.2, f32[1,1,1,3584,512]{4,3,2,1,0:T(8,128)S(1)} %bitcast.45, bf16[1,1,2,3584,512]{4,3,2,1,0:T(8,128)(2,1)} %param.12, pred[]{:T(512)} %bitcast.3, f32[1280,512]{1,0:T(8,128)S(1)} %fusion.8), kind=kOutput, calls=%fused_computation.23 | convolution fusion | flops 4708892672 | bytes 24117760 | tf_op jit(solution)/shard_map/dot_general | solution.py:51
  303.6 5.2 convolution_convert_fusion
  308.8 203.2 %all_to_all.21 = bf16[4,8,40,3584]{3,2,1,0:T(8,128)(2,1)} all-to-all(bf16[4,8,40,3584]{3,2,1,0:T(8,128)(2,1)S(1)} %bitcast.44), channel_id=1, replica_groups=mesh['grp'=4,'ex'=8] {'grp'}, dimensions={0} | all-to-all | bytes 18350080 | tf_op jit(solution)/shard_map/all_to_all | solution.py:56
  512.0 8.1 %copy.49 = bf16[4,8,40,3584]{3,2,0,1:T(8,128)(2,1)} copy(bf16[4,8,40,3584]{3,2,1,0:T(8,128)(2,1)} %all_to_all.21) | data formatting | bytes 18350080 | tf_op jit(solution)/shard_map/all_to_all | solution.py:56
  520.0 5.4 all-to-all-start.3
  525.8 102.1 %all-to-all-done.3 = bf16[4,8,40,3584]{3,2,0,1:T(8,128)(2,1)} async-done(((bf16[4,8,40,3584]{3,2,0,1:T(8,128)(2,1)}), bf16[4,8,40,3584]{3,2,0,1:T(8,128)(2,1)}, u32[]{:S(2)}, u32[]{:S(2)}) %all-to-all-start.3) | async-done | bytes 9175072 | tf_op jit(solution)/shard_map/all_to_all | solution.py:59
  627.9 8.0 %copy.50 = bf16[4,8,40,3584]{3,2,1,0:T(8,128)(2,1)} copy(bf16[4,8,40,3584]{3,2,0,1:T(8,128)(2,1)} %all-to-all-done.3) | data formatting | bytes 18350080 | tf_op jit(solution)/shard_map/all_to_all | solution.py:59
  635.8 12.7 %gather_fusion.1 = bf16[512,3584]{1,0:T(8,128)(2,1)} fusion(bf16[1280,3584]{1,0:T(8,128)(2,1)} %bitcast.40, s32[1024]{0:T(1024)S(1)} %pad_clamp_fusion.1), kind=kCustom, calls=%fused_computation.1 | custom fusion | bytes 7342080 | tf_op jit(solution)/shard_map/gather | solution.py:63
  648.5 12.7 %gather_fusion.2 = bf16[512,3584]{1,0:T(8,128)(2,1)} fusion(bf16[1280,3584]{1,0:T(8,128)(2,1)} %bitcast.41, s32[1024]{0:T(1024)S(1)} %pad_clamp_fusion), kind=kCustom, calls=%fused_computation.2 | custom fusion | bytes 7342080 | tf_op jit(solution)/shard_map/gather | solution.py:63
  661.2 4.1 add_convert_fusion
  665.3 3.8 bitcast_reduce_fusion
  (32 shorter events, 1.3 us)
Async XLA Ops:
  0.0 1.8 copy-start
  76.9 6.1 copy-start.6
  76.9 7.4 %copy-start.4 = (f32[1,1,4,3584]{3,2,1,0:T(4,128)S(1)}, f32[1,1,4,3584]{3,2,1,0:T(4,128)}, u32[]{:S(2)}) copy-start(f32[1,1,4,3584]{3,2,1,0:T(4,128)} %param.15) | copy-start | bytes 172036
  76.9 205.9 %all-to-all-start.1 = ((bf16[4,8,40,3584]{3,2,1,0:T(8,128)(2,1)}), bf16[4,8,40,3584]{3,2,1,0:T(8,128)(2,1)}, u32[]{:S(2)}, u32[]{:S(2)}) async-start(bf16[4,8,40,3584]{3,2,1,0:T(8,128)(2,1)} %bitcast.42), calls=%async_computation.1 | async-start | bytes 18350080 | tf_op jit(solution)/shard_map/all_to_all | solution.py:48
  84.3 4.8 copy-start.3
  293.3 10.3 %copy-start.2 = (bf16[512,3584]{1,0:T(8,128)(2,1)S(1)}, bf16[512,3584]{1,0:T(8,128)(2,1)}, u32[]{:S(2)}) copy-start(bf16[512,3584]{1,0:T(8,128)(2,1)} %fusion.3) | copy-start | bytes 11010052
  520.0 5.5 copy-start.5
  520.0 107.8 %all-to-all-start.3 = ((bf16[4,8,40,3584]{3,2,0,1:T(8,128)(2,1)}), bf16[4,8,40,3584]{3,2,0,1:T(8,128)(2,1)}, u32[]{:S(2)}, u32[]{:S(2)}) async-start(bf16[4,8,40,3584]{3,2,0,1:T(8,128)(2,1)} %copy.49), calls=%async_computation.3 | async-start | bytes 18350080 | tf_op jit(solution)/shard_map/all_to_all | solution.py:59
  661.2 7.9 %copy-start.1 = (bf16[64,3584]{1,0:T(8,128)(2,1)S(1)}, bf16[64,3584]{1,0:T(8,128)(2,1)}, u32[]{:S(2)}) copy-start(bf16[64,3584]{1,0:T(8,128)(2,1)} %param.8) | copy-start | bytes 1376260
where the time goes:
time: 670 us; the launch traced here: 669 us
  waiting for transfers between devices  296 us (44%)
  blocking collectives  261 us (39%)
  local copies, waits for them, and re-layouts  59.4 us (9%)
  matrix products  24.1 us (4%)
  other arithmetic  16.1 us (2%)
  starting transfers between devices  11.4 us (2%)
    all_to_all x1, blocking collectives, shards(): lax.all_to_all(partial_value.reshape(arrived_block.shape), 'grp', split_a...  203 us
    all_to_all x1, waiting for transfers between devices, shards(): lax.all_to_all(doubled, 'grp', split_axis=0, concat_axis=0, tiled=True)  194 us
    all_to_all x1, waiting for transfers between devices, shards(): lax.all_to_all(across, 'ex', split_axis=1, concat_axis=1, tiled=True)  102 us
    all_to_all x1, blocking collectives, shards(): lax.all_to_all(outgoing, 'ex', split_axis=1, concat_axis=1, tiled=True)  58.2 us
  transfers between devices with their start and end apart: 2, of which 2 were waited for; matrix products, arithmetic and copies ran while one was open for 1% of the time, Pallas kernels for 0%

commit v1 on v0

--- a/solution.py
+++ b/solution.py
@@ -11,7 +11,7 @@
     return jnp.where(is_hot, weights, scaled)
 
 
-def shards(
+def routed_shards(
     tokens, expert_ids, combine, hot_flags, gate_up_weight, gate_up_scale, down_weight, down_scale
 ):
     group_count = lax.axis_size("grp")
@@ -70,6 +70,50 @@
     )
 
 
+def dense_shards(
+    tokens, expert_ids, combine, hot_flags, gate_up_weight, gate_up_scale, down_weight, down_scale
+):
+    lane_count = lax.axis_size("ex")
+    expert_count = lax.axis_size("grp") // 2 * lane_count
+    own_expert = lax.axis_index("grp") // 2 * lane_count + lax.axis_index("ex")
+    is_hot = hot_flags[own_expert] == 1
+    named = expert_ids[:, :, None] == jnp.arange(expert_count, dtype=jnp.int32)
+    coefficient = jnp.sum(jnp.where(named, combine[:, :, None], 0.0), axis=1)
+    all_tokens = lax.all_gather(tokens, ("grp", "ex"), axis=0, tiled=True)
+    all_coefficient = lax.all_gather(coefficient, ("grp", "ex"), axis=0, tiled=True)
+    own_column = jnp.arange(expert_count, dtype=jnp.int32) == own_expert
+    weight = jnp.sum(jnp.where(own_column[None, :], all_coefficient, 0.0), axis=1)
+    gate_matrix = dequantize(gate_up_weight[0, 0, 0], gate_up_scale[0, 0, 0], is_hot)
+    up_matrix = dequantize(gate_up_weight[0, 0, 1], gate_up_scale[0, 0, 1], is_hot)
+    down_matrix = dequantize(down_weight[0, 0], down_scale[0, 0], is_hot)
+    gate_proj = jnp.dot(all_tokens, gate_matrix, preferred_element_type=jnp.float32)
+    up_proj = jnp.dot(all_tokens, up_matrix, preferred_element_type=jnp.float32)
+    hidden = (jax.nn.silu(gate_proj) * up_proj).astype(jnp.bfloat16)
+    partial_value = jnp.dot(hidden, down_matrix, preferred_element_type=jnp.float32)
+    routed = weight[:, None] != 0.0
+    scaled = jnp.where(routed, partial_value * weight[:, None], 0.0).astype(jnp.bfloat16)
+    lane_sum = lax.psum_scatter(
+        scaled.reshape(lax.axis_size("grp"), lane_count, tokens.shape[0], -1),
+        "ex",
+        scatter_dimension=1,
+        tiled=False,
+    )
+    return lax.psum_scatter(lane_sum, "grp", scatter_dimension=0, tiled=False)
+
+
+def shards(tokens, expert_ids, *rest):
+    group_count = lax.axis_size("grp")
+    lane_count = lax.axis_size("ex")
+    token_count = tokens.shape[0]
+    expert_count = group_count // 2 * lane_count
+    route_count = token_count * expert_ids.shape[1]
+    capacity = max(2, (5 * route_count + 4 * expert_count - 1) // (4 * expert_count))
+    chip_rows = group_count * lane_count // 2 * token_count
+    if 2 * expert_count * capacity >= chip_rows:
+        return dense_shards(tokens, expert_ids, *rest)
+    return routed_shards(tokens, expert_ids, *rest)
+
+
 def solution(mesh):
     return jax.shard_map(
         shards,

time: 670 us -> 320 us (0.48)
  blocking collectives: 261 us -> 45.1 us
  waiting for transfers between devices: 296 us -> 199 us
  local copies, waits for them, and re-layouts: 59.4 us -> 15.1 us
  between operations: 0.88 us -> 14.2 us
  matrix products: 24.1 us -> 36.9 us
  starting transfers between devices: 11.4 us -> 0.08 us
  other arithmetic: 16.1 us -> 9.34 us
    all_to_all x2 -> x0, waiting for transfers between devices: 296 us -> none  [the longest x1 194 us: shards(): lax.all_to_all(doubled, 'grp', split_axis=0, concat_axis=0, tiled=True)]
    all_to_all x2 -> x0, blocking collectives: 261 us -> none  [the longest x1 203 us: shards(): lax.all_to_all(partial_value.reshape(arrived_block.shape), 'grp', split_a...]
    reduce_scatter x0 -> x2, waiting for transfers between devices: none -> 145 us  [the longest x1 103 us: dense_shards(): lax.psum_scatter(scaled.reshape(lax.axis_size('grp'), lane_count, tokens....]
    all_gather x0 -> x1, waiting for transfers between devices: none -> 53.4 us  [dense_shards(): all_tokens = lax.all_gather(tokens, ('grp', 'ex'), axis=0, tiled=True)]
    all_gather x0 -> x1, blocking collectives: none -> 45.1 us  [dense_shards(): lax.all_gather(coefficient, ('grp', 'ex'), axis=0, tiled=True)]
    gather x3 -> x0, local copies, waits for them, and re-layouts: 30.5 us -> none  [the longest x1 12.7 us: shards(): flat_back[second_index].astype(jnp.float32)]
    all_to_all x3 -> x0, local copies, waits for them, and re-layouts: 18.5 us -> none  [the longest x1 8.05 us: shards(): lax.all_to_all(partial_value.reshape(arrived_block.shape), 'grp', split_a...]
    reshape x2 -> x1, local copies, waits for them, and re-layouts: 0.18 us -> 13.4 us  [dense_shards(): scaled.reshape(lax.axis_size('grp'), lane_count, tokens.shape[0], -1)]
  transfers between devices with their start and end apart: 2 -> 3, of which waited for: 2 -> 3; matrix products, arithmetic and copies ran while one was open for 1% -> 3% of each run, Pallas kernels for 0% -> 0%
where the time goes in v1:
time: 320 us
  waiting for transfers between devices  199 us (62%)
  blocking collectives  45.1 us (14%)
  matrix products  36.9 us (12%)
  local copies, waits for them, and re-layouts  15.1 us (5%)
  between operations  14.2 us (4%)
  other arithmetic  9.34 us (3%)
    reduce_scatter x1, waiting for transfers between devices, dense_shards(): lax.psum_scatter(scaled.reshape(lax.axis_size('grp'), lane_count, tokens....  103 us
    all_gather x1, waiting for transfers between devices, dense_shards(): all_tokens = lax.all_gather(tokens, ('grp', 'ex'), axis=0, tiled=True)  53.4 us
    all_gather x1, blocking collectives, dense_shards(): lax.all_gather(coefficient, ('grp', 'ex'), axis=0, tiled=True)  45.1 us
    reduce_scatter x1, waiting for transfers between devices, dense_shards(): return lax.psum_scatter(lane_sum, 'grp', scatter_dimension=0, tiled=False)  41.8 us
    dot_general x1, matrix products, dense_shards(): jnp.dot(hidden, down_matrix, preferred_element_type=jnp.float32)  23.3 us
    dot_general x1, matrix products, dense_shards(): jnp.dot(all_tokens, gate_matrix, preferred_element_type=jnp.float32)  13.6 us
    reshape x1, local copies, waits for them, and re-layouts, dense_shards(): scaled.reshape(lax.axis_size('grp'), lane_count, tokens.shape[0], -1)  13.4 us
    select_n x2, other arithmetic, dequantize(): return jnp.where(is_hot, weights, scaled)  8.51 us
  transfers between devices with their start and end apart: 3, of which 3 were waited for; matrix products, arithmetic and copies ran while one was open for 3% of the time, Pallas kernels for 0%

profile of v1, /device:TPU:0, one launch (start us, length us, event | category | flops | bytes accessed | tf_op | source)
XLA Modules:
  0.0 319.8 jit_solution(4791981176478052061)
XLA Ops:
  6.5 0.0 all-gather.3.cloned.1.call-start
  6.5 0.7 all-gather.3.cloned.1.call-update
  7.3 0.0 reduce-scatter.3.cloned.1.call-start
  7.3 0.7 select_reduce_fusion.1
  8.0 45.1 %all-gather = f32[32,64,16]{1,2,0:T(8,128)S(1)} all-gather(f32[1,64,16]{1,2,0:T(8,128)S(1)} %bitcast.65), channel_id=1, replica_groups=mesh['grp'=4,'ex'=8] {'grp','ex'}, dimensions={0}, use_global_device_ids=true | all-gather | bytes 135168 | tf_op jit(solution)/shard_map/all_gather | solution.py:83
  53.1 0.1 copy.28
  53.2 0.1 reshape.30
  53.4 0.0 copy-start
  53.4 1.4 dynamic_slice.3
  55.8 4.7 %fusion.5 = bf16[512,3584]{1,0:T(8,128)(2,1)} fusion(bf16[1,1,512,3584]{3,2,1,0:T(8,128)(2,1)} %param.14, f32[4,3584]{1,0:T(4,128)} %bitcast.64, pred[]{:T(512)} %bitcast.1), kind=kLoop, calls=%fused_computation.9 | loop fusion | flops 7340032 | bytes 7397377 | tf_op jit(solution)/shard_map/jit(_where)/select_n | solution.py:11
  60.5 0.0 copy-done.1
  60.5 0.1 fusion.11
  60.6 0.0 copy-done
  60.6 3.8 %fusion.4 = (bf16[3584,512]{1,0:T(8,128)(2,1)}, bf16[3584,512]{1,0:T(8,128)(2,1)}) fusion(f32[28,512]{1,0:T(8,128)S(1)} %get-tuple-element.9, bf16[1,1,2,3584,512]{4,3,2,1,0:T(8,128)(2,1)S(1)} %copy-done, pred[]{:T(512)} %bitcast.1, f32[28,512]{1,0:T(8,128)S(1)} %get-tuple-element.10), kind=kLoop, calls=%fused_computation.8 | loop fusion | flops 14680064 | bytes 14794753 | tf_op jit(solution)/shard_map/jit(_where)/select_n | solution.py:11
  64.4 0.1 select_reduce_fusion
  64.6 53.4 %all-gather.3.cloned.1.call-done = bf16[2048,3584]{1,0:T(8,128)(2,1)} async-done(((bf16[64,3584]{1,0:T(8,128)(2,1)}), bf16[2048,3584]{1,0:T(8,128)(2,1)}) %all-gather.3.cloned.1.call-update) | async-done | bytes 14680080 | tf_op jit(solution)/shard_map/all_gather | solution.py:82
  117.9 13.6 %fusion.12 = f32[512,2048]{1,0:T(8,128)} fusion(bf16[3584,512]{1,0:T(8,128)(2,1)} %get-tuple-element.6, bf16[2048,3584]{1,0:T(8,128)(2,1)} %all-gather.3.cloned.1.call-done), kind=kOutput, calls=%fused_computation.26 | convolution fusion | flops 7516192768 | bytes 22544384 | tf_op jit(solution)/shard_map/dot_general | solution.py:89
  131.5 23.3 %select_convert_fusion = bf16[2048,3584]{1,0:T(8,128)(2,1)} fusion(bf16[512,3584]{1,0:T(8,128)(2,1)} %fusion.5, f32[2048]{0:T(1024)S(1)} %select_reduce_fusion, pred[2048]{0:T(1024)(128)(4,1)S(1)} %broadcast_compare_fusion, f32[512,2048]{1,0:T(8,128)} %fusion.12, bf16[3584,512]{1,0:T(8,128)(2,1)} %get-tuple-element.5, ...), kind=kOutput, calls=%fused_computation | convolution fusion | flops 15060697088 | bytes 40904704 | tf_op jit(solution)/shard_map/dot_general | solution.py:92
  154.8 13.4 %copy.31 = bf16[4,8,64,3584]{3,2,0,1:T(8,128)(2,1)} copy(bf16[4,8,64,3584]{3,2,1,0:T(8,128)(2,1)} %bitcast.62) | data formatting | bytes 29360128 | tf_op jit(solution)/shard_map/reshape | solution.py:96
  168.3 0.0 reduce-scatter.3.cloned.1.call-update
  168.3 0.0 reduce-scatter.5.cloned.1.call-start
  168.4 103.1 %reduce-scatter.3.cloned.1.call-done = bf16[4,1,64,3584]{3,2,0,1:T(8,128)(2,1)} async-done(((bf16[4,8,64,3584]{3,2,0,1:T(8,128)(2,1)}), bf16[4,1,64,3584]{3,2,0,1:T(8,128)(2,1)}) %reduce-scatter.3.cloned.1.call-update) | async-done | bytes 1835024 | tf_op jit(solution)/shard_map/reduce_scatter | solution.py:95
  271.4 0.0 reduce-scatter.5.cloned.1.call-update
  271.5 41.8 %reduce-scatter.5.cloned.1.call-done = bf16[1,64,3584]{2,1,0:T(8,128)(2,1)} async-done(((bf16[4,64,3584]{2,1,0:T(8,128)(2,1)}), bf16[1,64,3584]{2,1,0:T(8,128)(2,1)}) %reduce-scatter.5.cloned.1.call-update) | async-done | bytes 458768 | tf_op jit(solution)/shard_map/reduce_scatter | solution.py:101
  (4 shorter events, 0.0 us)
Async XLA Ops:
  6.5 111.4 %all-gather.3.cloned.1.call-start = ((), (), s32[]{:S(2)}) async-start(), calls=%async_computation.2 | async-start | bytes 15138816 | tf_op jit(solution)/shard_map/all_gather | solution.py:82
  7.3 264.2 %reduce-scatter.3.cloned.1.call-start = ((), (), s32[]{:S(2)}) async-start(), calls=%async_computation.3 | async-start | bytes 16515072 | tf_op jit(solution)/shard_map/reduce_scatter | solution.py:95
  53.1 7.3 %copy-start.1 = (f32[1,1,2,28,512]{4,2,3,1,0:T(2,128)S(1)}, f32[1,1,2,28,512]{4,2,3,1,0:T(2,128)}, u32[]{:S(2)}) copy-start(f32[1,1,2,28,512]{4,2,3,1,0:T(2,128)} %param.13) | copy-start | bytes 344068
  53.4 7.2 %copy-start = (bf16[1,1,2,3584,512]{4,3,2,1,0:T(8,128)(2,1)S(1)}, bf16[1,1,2,3584,512]{4,3,2,1,0:T(8,128)(2,1)}, u32[]{:S(2)}) copy-start(bf16[1,1,2,3584,512]{4,3,2,1,0:T(8,128)(2,1)} %param.12) | copy-start | bytes 22020100
  168.3 145.0 %reduce-scatter.5.cloned.1.call-start = ((), (), s32[]{:S(2)}) async-start(), calls=%async_computation.4 | async-start | bytes 2293760 | tf_op jit(solution)/shard_map/reduce_scatter | solution.py:101
Sparse Core Ops, SparseCore 0:
  10.2 107.6 all-gather.2
  168.4 102.9 reduce-scatter.2
  273.8 39.4 reduce-scatter.4

commit v2 on v0

--- a/solution.py
+++ b/solution.py
@@ -1,6 +1,10 @@
+import functools
+
 import jax
 import jax.numpy as jnp
 from jax import lax
+from jax.experimental import pallas as pl
+from jax.experimental.pallas import tpu as pltpu
 from jax.sharding import PartitionSpec as P
 
 
@@ -11,7 +15,7 @@
     return jnp.where(is_hot, weights, scaled)
 
 
-def shards(
+def routed_shards(
     tokens, expert_ids, combine, hot_flags, gate_up_weight, gate_up_scale, down_weight, down_scale
 ):
     group_count = lax.axis_size("grp")
@@ -70,6 +74,376 @@
     )
 
 
+def fused_kernel(
+    planes,
+    experts,
+    own_ref,
+    gate_up_ref,
+    gate_up_scale_ref,
+    down_ref,
+    down_scale_ref,
+    out_ref,
+    rows_in,
+    parts,
+    core_in,
+    pair_in,
+    last_in,
+    plane_in,
+    gate_up,
+    down,
+    hidden,
+    load_sem,
+    plane_sems,
+    spread_sems,
+    twin_sems,
+    core_sems,
+    pair_sems,
+    last_sems,
+    back_sems,
+):
+    f32, bf16 = jnp.float32, jnp.bfloat16
+    rows, width = out_ref.shape
+    half = rows // 2
+    units = hidden.shape[1]
+    z = lax.axis_index("grp")
+    lane = lax.axis_index("ex")
+    core = lane % 2
+    x = (lane // 2) % 2
+    y = lane // 4
+    expert = z // 2 * lax.axis_size("ex") + lane
+    across_x = {"ex": lane + 2 - 4 * x}
+    across_y = {"ex": lane + 4 - 8 * y}
+    twin = {"ex": lane + 1 - 2 * core}
+    neighbours = [across_x, across_y, twin]
+    neighbours += [{"grp": lax.rem(z + step, planes)} for step in range(1, planes)]
+    own_rows = pl.ds(pl.multiple_of(core * rows, rows), rows)
+    twin_rows = pl.ds(pl.multiple_of((1 - core) * rows, rows), rows)
+    half_rows = [pl.ds(pl.multiple_of(core * rows + t * half, half), half) for t in range(2)]
+
+    barrier = pltpu.get_barrier_semaphore()
+    for neighbour in neighbours:
+        pl.semaphore_signal(
+            barrier, inc=1, device_id=neighbour, device_id_type=pl.DeviceIdType.MESH
+        )
+    pl.semaphore_wait(barrier, len(neighbours))
+
+    pending = []
+
+    def send(source, target, sems, index, device):
+        copy = pltpu.make_async_remote_copy(
+            src_ref=source,
+            dst_ref=target,
+            send_sem=sems.at[(0,) + index],
+            recv_sem=sems.at[(1,) + index],
+            device_id=device,
+            device_id_type=pl.DeviceIdType.MESH,
+        )
+        copy.start()
+        pending.append(copy)
+        return copy
+
+    own_copy = pltpu.make_async_copy(own_ref, rows_in.at[0, y, x, own_rows], load_sem.at[0])
+    own_copy.start()
+    loads = [
+        pltpu.make_async_copy(gate_up_ref.at[0], gate_up.at[0], load_sem.at[1]),
+        pltpu.make_async_copy(gate_up_ref.at[1], gate_up.at[1], load_sem.at[2]),
+        pltpu.make_async_copy(down_ref, down, load_sem.at[3]),
+    ]
+    from_plane = {}
+    for k in range(1, planes):
+        from_plane[k] = send(
+            own_ref,
+            rows_in.at[k, y, x, own_rows],
+            plane_sems,
+            (k,),
+            {"grp": lax.rem(z + planes - k, planes)},
+        )
+    own_copy.wait()
+    for load in loads:
+        load.start()
+
+    spread = {}
+
+    def first_spread(k):
+        if k >= planes:
+            return
+        if k > 0:
+            from_plane[k].wait_recv()
+        for t in range(2):
+            block = rows_in.at[k, y, x, half_rows[t]]
+            first, second = (across_x, across_y) if t == 0 else (across_y, across_x)
+            spread[k, t, 0] = send(block, block, spread_sems, (k, t, 0), first)
+            spread[k, t, 1] = send(block, block, spread_sems, (k, t, 1), second)
+
+    def second_spread(k):
+        if k >= planes:
+            return
+        for t in range(2):
+            spread[k, t, 0].wait_recv()
+            if t == 0:
+                block, second = rows_in.at[k, y, 1 - x, half_rows[t]], across_y
+            else:
+                block, second = rows_in.at[k, 1 - y, x, half_rows[t]], across_x
+            spread[k, t, 2] = send(block, block, spread_sems, (k, t, 2), second)
+
+    twins = {}
+
+    def to_twin(k):
+        if k >= planes:
+            return
+        for t in range(2):
+            spread[k, t, 1].wait_recv()
+            spread[k, t, 2].wait_recv()
+        block = rows_in.at[k, :, :, own_rows]
+        twins[k] = send(block, block, twin_sems, (k,), twin)
+
+    def gate_up_phase(k, part):
+        tile = min(units, 256)
+
+        def columns_of(n, carry):
+            at = pl.ds(pl.multiple_of(n * tile, tile), tile)
+            block = rows_in[k, part, :, :, :width].reshape(hidden.shape[0], width)
+            gate = jnp.dot(block, gate_up[0, :, at], preferred_element_type=f32)
+            up = jnp.dot(block, gate_up[1, :, at], preferred_element_type=f32)
+            hidden[:, at] = (gate / (1.0 + jnp.exp(-gate)) * up).astype(bf16)
+            return carry
+
+        lax.fori_loop(0, units // tile, columns_of, 0)
+
+    def down_phase(k, part):
+        tile = 512 if width % 512 == 0 else 128
+        extra = rows_in[k, part, :, :, width:].reshape(hidden.shape[0], -1).astype(f32)
+        column = lax.broadcasted_iota(jnp.int32, extra.shape, 1)
+        chosen = (
+            (column == expert) | (column == expert + experts) | (column == expert + 2 * experts)
+        )
+        weight = jnp.sum(jnp.where(chosen, extra, 0.0), axis=1, keepdims=True)
+
+        def columns_of(n, carry):
+            at = pl.ds(pl.multiple_of(n * tile, tile), tile)
+            value = jnp.dot(hidden[...], down[:, at], preferred_element_type=f32)
+            value = jnp.where(weight != 0.0, value * weight, 0.0).astype(bf16)
+            parts[k, part, :, :, at] = value.reshape(2, 2 * rows, tile)
+            return carry
+
+        lax.fori_loop(0, width // tile, columns_of, 0)
+
+    step = 16
+
+    def add_rows(count, target, source):
+        def one(i, carry):
+            at_target, at_source = target(i), source(i)
+            total = parts[at_target].astype(f32) + at_source[0][at_source[1]].astype(f32)
+            parts[at_target] = total.astype(bf16)
+            return carry
+
+        lax.fori_loop(0, count, one, 0)
+
+    returns = {}
+
+    def return_core(k):
+        returns[k, "core"] = send(
+            parts.at[k, :, :, twin_rows], core_in.at[k], core_sems, (k,), twin
+        )
+
+    def return_pair(k):
+        if k < 0:
+            return
+        returns[k, "core"].wait_recv()
+        per = rows // step
+
+        def target(i):
+            at = pl.ds(pl.multiple_of(core * rows + i % per * step, step), step)
+            return (k, i // per // 2, i // per % 2, at)
+
+        def source(i):
+            at = pl.ds(pl.multiple_of(i % per * step, step), step)
+            return core_in, (k, i // per // 2, i // per % 2, at)
+
+        add_rows(4 * per, target, source)
+        returns[k, "a"] = send(
+            parts.at[k, 1 - y, :, half_rows[0]], pair_in.at[k, 0], pair_sems, (k, 0), across_y
+        )
+        returns[k, "b"] = send(
+            parts.at[k, :, 1 - x, half_rows[1]], pair_in.at[k, 1], pair_sems, (k, 1), across_x
+        )
+
+    def return_last(k):
+        if k < 0:
+            return
+        per = half // step
+        for t in range(2):
+            returns[k, "ab"[t]].wait_recv()
+
+            def target(i, t=t):
+                at = pl.ds(pl.multiple_of(core * rows + t * half + i % per * step, step), step)
+                return (k, y, i // per, at) if t == 0 else (k, i // per, x, at)
+
+            def source(i, t=t):
+                at = pl.ds(pl.multiple_of(i % per * step, step), step)
+                return pair_in, (k, t, i // per, at)
+
+            add_rows(2 * per, target, source)
+        returns[k, "c"] = send(
+            parts.at[k, y, 1 - x, half_rows[0]], last_in.at[k, 0], last_sems, (k, 0), across_x
+        )
+        returns[k, "d"] = send(
+            parts.at[k, 1 - y, x, half_rows[1]], last_in.at[k, 1], last_sems, (k, 1), across_y
+        )
+
+    def return_plane(k):
+        if k < 0:
+            return
+        per = half // step
+        for t in range(2):
+            returns[k, "cd"[t]].wait_recv()
+
+            def target(i, t=t):
+                at = pl.ds(pl.multiple_of(core * rows + t * half + i * step, step), step)
+                return (k, y, x, at)
+
+            def source(i, t=t):
+                at = pl.ds(pl.multiple_of(i * step, step), step)
+                return last_in, (k, t, at)
+
+            add_rows(per, target, source)
+        if k > 0:
+            returns[k, "z"] = send(
+                parts.at[k, y, x, own_rows],
+                plane_in.at[k],
+                back_sems,
+                (k,),
+                {"grp": lax.rem(z + k, planes)},
+            )
+
+    def scale_rows(ref, scales, pick):
+        groups = scales.shape[0]
+        size = ref.shape[0] // groups
+
+        def one(g, carry):
+            at = pl.ds(pl.multiple_of(g * size, size), size)
+            ref[at] = (ref[at].astype(f32) * scales[pl.ds(g, 1), :]).astype(bf16)
+            return carry
+
+        lax.fori_loop(0, groups, one, 0)
+
+    first_spread(0)
+    loads[0].wait()
+    scale_rows(gate_up.at[0], gate_up_scale_ref.at[0], 0)
+    second_spread(0)
+    first_spread(1)
+    loads[1].wait()
+    scale_rows(gate_up.at[1], gate_up_scale_ref.at[1], 0)
+    loads[2].wait()
+    scale_rows(down, down_scale_ref, 0)
+    to_twin(0)
+
+    for k in range(planes):
+        second_spread(k + 1)
+        first_spread(k + 2)
+        twins[k].wait_recv()
+        gate_up_phase(k, 0)
+        return_pair(k - 1)
+        down_phase(k, 0)
+        return_last(k - 1)
+        gate_up_phase(k, 1)
+        down_phase(k, 1)
+        return_plane(k - 1)
+        to_twin(k + 1)
+        return_core(k)
+    return_pair(planes - 1)
+    return_last(planes - 1)
+    return_plane(planes - 1)
+    for k in range(1, planes):
+        returns[k, "z"].wait_recv()
+
+    def finish(i, carry):
+        at = pl.ds(pl.multiple_of(i * step, step), step)
+        mine = pl.ds(pl.multiple_of(core * rows + i * step, step), step)
+        total = parts[0, y, x, mine].astype(f32)
+        for k in range(1, planes):
+            total = total + plane_in[k, at].astype(f32)
+        out_ref[at] = total.astype(bf16)
+        return carry
+
+    lax.fori_loop(0, rows // step, finish, 0)
+    for copy in pending:
+        copy.wait_send()
+
+
+def dense_shards(
+    tokens, expert_ids, combine, hot_flags, gate_up_weight, gate_up_scale, down_weight, down_scale
+):
+    planes = lax.axis_size("grp")
+    lane_count = lax.axis_size("ex")
+    expert_count = planes // 2 * lane_count
+    rows, width = tokens.shape
+    units = down_weight.shape[2]
+    own_expert = lax.axis_index("grp") // 2 * lane_count + lax.axis_index("ex")
+    is_hot = hot_flags[own_expert] == 1
+    named = expert_ids[:, :, None] == jnp.arange(expert_count, dtype=jnp.int32)
+    coefficient = jnp.sum(jnp.where(named, combine[:, :, None], 0.0), axis=1)
+    pieces, rest = [], coefficient
+    for _ in range(3):
+        piece = lax.reduce_precision(rest, 8, 7)
+        pieces.append(piece.astype(jnp.bfloat16))
+        rest = rest - piece
+    extra = -(-3 * expert_count // 128) * 128
+    blank = jnp.zeros((rows, extra - 3 * expert_count), jnp.bfloat16)
+    own_rows = jnp.concatenate([tokens] + pieces + [blank], axis=1)
+    gate_up_factor = jnp.where(is_hot, 1.0, gate_up_scale[0, 0])
+    down_factor = jnp.where(is_hot, 1.0, down_scale[0, 0])
+    bf16 = jnp.bfloat16
+    dma = pltpu.SemaphoreType.DMA
+    return pl.pallas_call(
+        functools.partial(fused_kernel, planes, expert_count),
+        out_shape=jax.ShapeDtypeStruct((rows, width), bf16),
+        in_specs=[
+            pl.BlockSpec(memory_space=pl.ANY),
+            pl.BlockSpec(memory_space=pl.ANY),
+            pl.BlockSpec(memory_space=pltpu.VMEM),
+            pl.BlockSpec(memory_space=pl.ANY),
+            pl.BlockSpec(memory_space=pltpu.VMEM),
+        ],
+        out_specs=pl.BlockSpec(memory_space=pltpu.VMEM),
+        scratch_shapes=[
+            pltpu.VMEM((planes, 2, 2, 2 * rows, width + extra), bf16),
+            pltpu.VMEM((planes, 2, 2, 2 * rows, width), bf16),
+            pltpu.VMEM((planes, 2, 2, rows, width), bf16),
+            pltpu.VMEM((planes, 2, 2, rows // 2, width), bf16),
+            pltpu.VMEM((planes, 2, rows // 2, width), bf16),
+            pltpu.VMEM((planes, rows, width), bf16),
+            pltpu.VMEM((2, width, units), bf16),
+            pltpu.VMEM((units, width), bf16),
+            pltpu.VMEM((4 * rows, units), bf16),
+            dma((4,)),
+            dma((2, planes)),
+            dma((2, planes, 2, 3)),
+            dma((2, planes)),
+            dma((2, planes)),
+            dma((2, planes, 2)),
+            dma((2, planes, 2)),
+            dma((2, planes)),
+        ],
+        compiler_params=pltpu.CompilerParams(
+            collective_id=0, has_side_effects=True, vmem_limit_bytes=67043328
+        ),
+    )(own_rows, gate_up_weight[0, 0], gate_up_factor, down_weight[0, 0], down_factor)
+
+
+def shards(tokens, expert_ids, *rest):
+    group_count = lax.axis_size("grp")
+    lane_count = lax.axis_size("ex")
+    token_count = tokens.shape[0]
+    expert_count = group_count // 2 * lane_count
+    route_count = token_count * expert_ids.shape[1]
+    capacity = max(2, (5 * route_count + 4 * expert_count - 1) // (4 * expert_count))
+    chip_rows = group_count * lane_count // 2 * token_count
+    if lane_count == 2 * 2 * 2 and 2 * expert_count * capacity >= chip_rows:
+        return dense_shards(tokens, expert_ids, *rest)
+    return routed_shards(tokens, expert_ids, *rest)
+
+
 def solution(mesh):
     return jax.shard_map(
         shards,

time: 670 us -> 181 us (0.27)
  waiting for transfers between devices: 296 us -> 0 us
  blocking collectives: 261 us -> 0 us
  Pallas kernels: 0 us -> 173 us
  local copies, waits for them, and re-layouts: 59.4 us -> 5.1 us
  matrix products: 24.1 us -> 0 us
  other arithmetic: 16.1 us -> 2.97 us
  starting transfers between devices: 11.4 us -> 0 us
    all_to_all x2 -> x0, waiting for transfers between devices: 296 us -> none  [the longest x1 194 us: shards(): lax.all_to_all(doubled, 'grp', split_axis=0, concat_axis=0, tiled=True)]
    all_to_all x2 -> x0, blocking collectives: 261 us -> none  [the longest x1 203 us: shards(): lax.all_to_all(partial_value.reshape(arrived_block.shape), 'grp', split_a...]
    pallas_call x0 -> x1, Pallas kernels: none -> 173 us  [dense_shards(): pl.pallas_call(functools.partial(fused_kernel, planes, expert_count), out...]
    gather x3 -> x0, local copies, waits for them, and re-layouts: 30.5 us -> none  [the longest x1 12.7 us: shards(): flat_back[second_index].astype(jnp.float32)]
    dot_general x3 -> x0, matrix products: 24.1 us -> none  [the longest x1 10.3 us: shards(): up_proj = jnp.dot(flat_rows, up_matrix, preferred_element_type=jnp.float32)]
    all_to_all x3 -> x0, local copies, waits for them, and re-layouts: 18.5 us -> none  [the longest x1 8.05 us: shards(): lax.all_to_all(partial_value.reshape(arrived_block.shape), 'grp', split_a...]
    all_to_all x2 -> x0, starting transfers between devices: 11.4 us -> none  [the longest x1 6.09 us: shards(): lax.all_to_all(doubled, 'grp', split_axis=0, concat_axis=0, tiled=True)]
  transfers between devices with their start and end apart: 2 -> 0, of which waited for: 2 -> 0; matrix products, arithmetic and copies ran while one was open for 1% -> 0% of each run, Pallas kernels for 0% -> 0%
where the time goes in v2:
time: 181 us
  Pallas kernels  173 us (96%)
  local copies, waits for them, and re-layouts  5.1 us (3%)
  other arithmetic  2.97 us (2%)
    pallas_call x1, Pallas kernels, dense_shards(): pl.pallas_call(functools.partial(fused_kernel, planes, expert_count), out...  173 us

profile of v2, /device:TPU:0, one launch (start us, length us, event | category | flops | bytes accessed | tf_op | source)
XLA Modules:
  0.0 181.5 jit_solution(2582536226014387053)
XLA Ops:
  0.0 1.2 dynamic_slice.3
  1.9 0.7 select_reduce_fusion
  2.6 0.1 copy.16
  2.7 0.1 copy.15
  2.8 0.7 select_bitcast_fusion.down_scale_ref
  3.5 1.6 fusion.gate_up_scale_ref
  5.1 1.9 %concatenate.3.own_ref = bf16[64,3712]{1,0:T(8,128)(2,1)} concatenate(bf16[64,3584]{1,0:T(8,128)(2,1)} %param.8, bf16[64,16]{1,0:T(8,128)(2,1)S(1)} %get-tuple-element.7, bf16[64,16]{1,0:T(8,128)(2,1)S(1)} %get-tuple-element.6, bf16[64,16]{1,0:T(8,128)(2,1)S(1)} %get-tuple-element.5, bf16[64,80]{1,0:T(8,128)(2,1)S(1)} %broadcast_in_dim.28), dimensions={1} | concatenate | bytes 950272 | tf_op jit(solution)/shard_map/concatenate | solution.py:393
  6.9 172.7 %shard_map.82 = bf16[64,3584]{1,0:T(8,128)(2,1)} custom-call(bf16[64,3712]{1,0:T(8,128)(2,1)} %concatenate.3.own_ref, bf16[2,3584,512]{2,1,0:T(8,128)(2,1)} %bitcast.7, f32[2,28,512]{2,1,0:T(8,128)} %fusion.gate_up_scale_ref, bf16[512,3584]{1,0:T(8,128)(2,1)} %bitcast.8, f32[4,3584]{1,0:T(4,128)} %select_bitcast_fusion.down_scale_ref), custom_call_target="tpu_custom_call" | custom-call | tf_op jit(solution)/shard_map/pallas_call | solution.py:398
  179.7 1.8 %copy.23 = bf16[64,3584]{1,0:T(8,128)(2,1)} copy(bf16[64,3584]{1,0:T(8,128)(2,1)} %shard_map.82) | data formatting | bytes 917504
  (3 shorter events, 0.0 us)

commit v3 on v2

--- a/solution.py
+++ b/solution.py
@@ -150,7 +150,10 @@
         pltpu.make_async_copy(down_ref, down, load_sem.at[3]),
     ]
     from_plane = {}
-    for k in range(1, planes):
+
+    def to_plane(k):
+        if k >= planes:
+            return
         from_plane[k] = send(
             own_ref,
             rows_in.at[k, y, x, own_rows],
@@ -158,6 +161,9 @@
             (k,),
             {"grp": lax.rem(z + planes - k, planes)},
         )
+
+    to_plane(1)
+    to_plane(2)
     own_copy.wait()
     for load in loads:
         load.start()
@@ -316,7 +322,7 @@
                 {"grp": lax.rem(z + k, planes)},
             )
 
-    def scale_rows(ref, scales, pick):
+    def scale_rows(ref, scales):
         groups = scales.shape[0]
         size = ref.shape[0] // groups
 
@@ -329,31 +335,42 @@
 
     first_spread(0)
     loads[0].wait()
-    scale_rows(gate_up.at[0], gate_up_scale_ref.at[0], 0)
+    scale_rows(gate_up.at[0], gate_up_scale_ref.at[0])
     second_spread(0)
     first_spread(1)
     loads[1].wait()
-    scale_rows(gate_up.at[1], gate_up_scale_ref.at[1], 0)
+    scale_rows(gate_up.at[1], gate_up_scale_ref.at[1])
     loads[2].wait()
-    scale_rows(down, down_scale_ref, 0)
+    scale_rows(down, down_scale_ref)
     to_twin(0)
+    second_spread(1)
 
     for k in range(planes):
-        second_spread(k + 1)
+        for later in range(k + 3, planes if k == 0 else k + 3):
+            to_plane(later)
         first_spread(k + 2)
+        if k > 2:
+            return_pair(k - 1)
         twins[k].wait_recv()
         gate_up_phase(k, 0)
-        return_pair(k - 1)
         down_phase(k, 0)
-        return_last(k - 1)
+        to_twin(k + 1)
+        second_spread(k + 2)
+        if k == planes - 1:
+            return_pair(0)
+            return_last(1)
         gate_up_phase(k, 1)
         down_phase(k, 1)
+        return_core(k)
+        if k == 2:
+            return_pair(1)
+    return_pair(planes - 1)
+    for k in range(2, planes):
+        return_last(k)
         return_plane(k - 1)
-        to_twin(k + 1)
-        return_core(k)
-    return_pair(planes - 1)
-    return_last(planes - 1)
+    return_last(0)
     return_plane(planes - 1)
+    return_plane(0)
     for k in range(1, planes):
         returns[k, "z"].wait_recv()
 

time: 181 us -> 170 us (0.939); the launches traced: 181 us -> 168 us
  Pallas kernels: 173 us -> 158 us
    pallas_call x1, Pallas kernels: 173 us -> 158 us  [dense_shards(): pl.pallas_call(functools.partial(fused_kernel, planes, expert_count), out...]
where the time goes in v3:
time: 170 us; the launch traced here: 168 us
  Pallas kernels  158 us (93%)
  local copies, waits for them, and re-layouts  5.1 us (3%)
  other arithmetic  3.79 us (2%)
    pallas_call x1, Pallas kernels, dense_shards(): pl.pallas_call(functools.partial(fused_kernel, planes, expert_count), out...  158 us

profile of v3, /device:TPU:0, one launch (start us, length us, event | category | flops | bytes accessed | tf_op | source)
XLA Modules:
  0.0 167.9 jit_solution(16798196873401790172)
XLA Ops:
  0.0 1.2 dynamic_slice.3
  1.9 0.7 select_reduce_fusion
  2.6 0.1 copy.16
  2.7 0.1 copy.15
  2.8 1.5 select_bitcast_fusion.down_scale_ref
  4.3 1.6 fusion.gate_up_scale_ref
  5.9 1.9 %concatenate.3.own_ref = bf16[64,3712]{1,0:T(8,128)(2,1)} concatenate(bf16[64,3584]{1,0:T(8,128)(2,1)} %param.8, bf16[64,16]{1,0:T(8,128)(2,1)S(1)} %get-tuple-element.7, bf16[64,16]{1,0:T(8,128)(2,1)S(1)} %get-tuple-element.6, bf16[64,16]{1,0:T(8,128)(2,1)S(1)} %get-tuple-element.5, bf16[64,80]{1,0:T(8,128)(2,1)S(1)} %broadcast_in_dim.28), dimensions={1} | concatenate | bytes 950272 | tf_op jit(solution)/shard_map/concatenate | solution.py:410
  7.7 158.4 %shard_map.82 = bf16[64,3584]{1,0:T(8,128)(2,1)} custom-call(bf16[64,3712]{1,0:T(8,128)(2,1)} %concatenate.3.own_ref, bf16[2,3584,512]{2,1,0:T(8,128)(2,1)} %bitcast.7, f32[2,28,512]{2,1,0:T(8,128)} %fusion.gate_up_scale_ref, bf16[512,3584]{1,0:T(8,128)(2,1)} %bitcast.8, f32[4,3584]{1,0:T(4,128)} %select_bitcast_fusion.down_scale_ref), custom_call_target="tpu_custom_call" | custom-call | tf_op jit(solution)/shard_map/pallas_call | solution.py:415
  166.1 1.8 %copy.23 = bf16[64,3584]{1,0:T(8,128)(2,1)} copy(bf16[64,3584]{1,0:T(8,128)(2,1)} %shard_map.82) | data formatting | bytes 917504
  (3 shorter events, 0.0 us)

commit v4 on v3

--- a/solution.py
+++ b/solution.py
@@ -77,6 +77,7 @@
 def fused_kernel(
     planes,
     experts,
+    hot_ref,
     own_ref,
     gate_up_ref,
     gate_up_scale_ref,
@@ -116,6 +117,7 @@
     twin = {"ex": lane + 1 - 2 * core}
     neighbours = [across_x, across_y, twin]
     neighbours += [{"grp": lax.rem(z + step, planes)} for step in range(1, planes)]
+    is_hot = hot_ref[expert] == 1
     own_rows = pl.ds(pl.multiple_of(core * rows, rows), rows)
     twin_rows = pl.ds(pl.multiple_of((1 - core) * rows, rows), rows)
     half_rows = [pl.ds(pl.multiple_of(core * rows + t * half, half), half) for t in range(2)]
@@ -328,7 +330,7 @@
 
         def one(g, carry):
             at = pl.ds(pl.multiple_of(g * size, size), size)
-            ref[at] = (ref[at].astype(f32) * scales[pl.ds(g, 1), :]).astype(bf16)
+            ref[at] = (ref[at].astype(f32) * jnp.where(is_hot, 1.0, scales[pl.ds(g, 1), :])).astype(bf16)
             return carry
 
         lax.fori_loop(0, groups, one, 0)
@@ -396,8 +398,6 @@
     expert_count = planes // 2 * lane_count
     rows, width = tokens.shape
     units = down_weight.shape[2]
-    own_expert = lax.axis_index("grp") // 2 * lane_count + lax.axis_index("ex")
-    is_hot = hot_flags[own_expert] == 1
     named = expert_ids[:, :, None] == jnp.arange(expert_count, dtype=jnp.int32)
     coefficient = jnp.sum(jnp.where(named, combine[:, :, None], 0.0), axis=1)
     pieces, rest = [], coefficient
@@ -408,14 +408,13 @@
     extra = -(-3 * expert_count // 128) * 128
     blank = jnp.zeros((rows, extra - 3 * expert_count), jnp.bfloat16)
     own_rows = jnp.concatenate([tokens] + pieces + [blank], axis=1)
-    gate_up_factor = jnp.where(is_hot, 1.0, gate_up_scale[0, 0])
-    down_factor = jnp.where(is_hot, 1.0, down_scale[0, 0])
     bf16 = jnp.bfloat16
     dma = pltpu.SemaphoreType.DMA
     return pl.pallas_call(
         functools.partial(fused_kernel, planes, expert_count),
         out_shape=jax.ShapeDtypeStruct((rows, width), bf16),
         in_specs=[
+            pl.BlockSpec(memory_space=pltpu.SMEM),
             pl.BlockSpec(memory_space=pl.ANY),
             pl.BlockSpec(memory_space=pl.ANY),
             pl.BlockSpec(memory_space=pltpu.VMEM),
@@ -445,7 +444,14 @@
         compiler_params=pltpu.CompilerParams(
             collective_id=0, has_side_effects=True, vmem_limit_bytes=67043328
         ),
-    )(own_rows, gate_up_weight[0, 0], gate_up_factor, down_weight[0, 0], down_factor)
+    )(
+        hot_flags,
+        own_rows,
+        gate_up_weight[0, 0],
+        gate_up_scale[0, 0],
+        down_weight[0, 0],
+        down_scale[0, 0],
+    )
 
 
 def shards(tokens, expert_ids, *rest):

time: 170 us -> 167 us (0.982)
  other arithmetic: 3.79 us -> 0.74 us
    select_n x2 -> x0, other arithmetic: 3.05 us -> none  [the longest x1 1.58 us: dense_shards(): gate_up_factor = jnp.where(is_hot, 1.0, gate_up_scale[0, 0])]
where the time goes in v4:
time: 167 us; the launch traced here: 165 us
  Pallas kernels  159 us (95%)
  local copies, waits for them, and re-layouts  5.44 us (3%)
    pallas_call x1, Pallas kernels, dense_shards(): pl.pallas_call(functools.partial(fused_kernel, planes, expert_count), out...  159 us
    unnamed x2, local copies, waits for them, and re-layouts  3.39 us

profile of v4, /device:TPU:0, one launch (start us, length us, event | category | flops | bytes accessed | tf_op | source)
XLA Modules:
  0.0 165.4 jit_solution(2862658799002035818)
XLA Ops:
  0.0 0.7 select_reduce_fusion
  0.7 0.1 copy.16
  0.8 0.1 copy.15
  0.9 1.6 copy.20
  2.5 1.9 %concatenate.3.own_ref = bf16[64,3712]{1,0:T(8,128)(2,1)} concatenate(bf16[64,3584]{1,0:T(8,128)(2,1)} %param.8, bf16[64,16]{1,0:T(8,128)(2,1)S(1)} %get-tuple-element.7, bf16[64,16]{1,0:T(8,128)(2,1)S(1)} %get-tuple-element.6, bf16[64,16]{1,0:T(8,128)(2,1)S(1)} %get-tuple-element.5, bf16[64,80]{1,0:T(8,128)(2,1)S(1)} %broadcast_in_dim.20), dimensions={1} | concatenate | bytes 950272 | tf_op jit(solution)/shard_map/concatenate | solution.py:410
  4.4 159.2 %shard_map.82 = bf16[64,3584]{1,0:T(8,128)(2,1)} custom-call(s32[16]{0:T(128)} %hot_ref.1, bf16[64,3712]{1,0:T(8,128)(2,1)} %concatenate.3.own_ref, bf16[2,3584,512]{2,1,0:T(8,128)(2,1)} %bitcast.6, f32[2,28,512]{2,1,0:T(8,128)} %bitcast.8, bf16[512,3584]{1,0:T(8,128)(2,1)} %bitcast.7, f32[4,3584]{1,0:T(4,128)} %bitcast.9), custom_call_target="tpu_custom_call" | custom-call | tf_op jit(solution)/shard_map/pallas_call | solution.py:413
  163.6 1.8 %copy.22 = bf16[64,3584]{1,0:T(8,128)(2,1)} copy(bf16[64,3584]{1,0:T(8,128)(2,1)} %shard_map.82) | data formatting | bytes 917504
  (3 shorter events, 0.0 us)
